TPU v7x, 32 devices: a whole 2x2x4 slice. The times are simulated.
32 devices in a mesh: member: 8 (over y, x, core), region: 4 (over z).
Axes of the slice: x: 2, y: 2, z: 4, core: 2. Of those that a mesh axis runs over, the one named last changes fastest.
Arguments:
- state: bfloat16 [16, 64, 4096], P('member', 'region'), may hold values from -6 to 6
- diffusivity: float32 [64, 4096], P('region'), may hold values from 0.05 to 0.45
- model_perturbation: bfloat16 [2, 16, 64, 4096], P(None, 'member', 'region'), may hold values from -3 to 3
- obs_values: float32 [2, 128, 16], P(None, 'region'), may hold values from -14 to 14
- obs_prec: float32 [128, 16], P('region'), may hold values from 0.5 to 2
- obs_tile: int32 [128], P('region'), may hold values from 0 to 15
- obs_cell: int32 [128, 16], P('region'), may hold values from 0 to 4095
- pattern: int32 [64, 6], P('region'), may hold values from 0 to 31
- loc_weight: float32 [64, 6], P('region'), may hold values from 0.02 to 0.2
- anc_member: int32 [2, 4, 16, 16, 1], P(None, 'region', 'member'), may hold values from 0 to 7; in each aligned block of 32 rows (0 to 31, 32 to 63, ..., all dimensions but the last counted through in order) at most 8 rows name the same one
- anc_slot: int32 [2, 4, 16, 16], P(None, 'region', 'member'), may hold values from 0 to 1
Outputs:
- analysis: bfloat16 [16, 64, 4096], P('member', 'region')
- analysis_mean: float32 [2, 64, 4096], P(None, 'region', 'member')
Inputs may be any that keep to these rules, and one draw needn't show every extreme that they name: `anc_member`: within one cycle, among the 32 particle tiles of one device (one member index, one region), at most 8 ancestors lie on the same member index.
All inputs are finite; a program needn't handle non-finite values.
Results may differ from a plain program's by a relative error of at most 0.0046.
Values may be sent and summed in bfloat16 or wider, within the bound.
No kernel may reach another device: no remote copies, remote signals or barrier semaphores. Data moves between devices by JAX's collectives and lax.ppermute only.
A program may use at most 64 MiB of HBM per device.

v0:
```python
import jax
import jax.numpy as jnp
from jax import lax
from jax.sharding import PartitionSpec as P

CYCLES = 2
STEPS = 2


def extended(array, sides, width):
    for axis, dim in sides:
        peers, length = (lax.axis_size(axis), array.shape[dim])
        up = [(i, (i + 1) % peers) for i in range(peers - 1)]
        down = [(j, i) for i, j in up]
        last = lax.slice_in_dim(array, length - width, length, axis=dim)
        initial = lax.slice_in_dim(array, 0, width, axis=dim)
        before = lax.ppermute(last, axis, up)
        after = lax.ppermute(initial, axis, down)
        array = jnp.concatenate([before, array, after], axis=dim)
    return array


def body(
    state,
    diffusivity,
    model_perturbation,
    obs_values,
    obs_prec,
    obs_tile,
    obs_cell,
    pattern,
    loc_weight,
    anc_member,
    anc_slot,
):
    part_dev, tiles_dev, patch_extent = state.shape
    members = lax.axis_size("member")
    capacity = max(2, 2 * part_dev * tiles_dev // members)
    area_members = part_dev * tiles_dev
    strip_extent = tiles_dev * patch_extent
    smoothed_strip = diffusivity.reshape(1, strip_extent)
    measured_position = obs_tile[:, None] * patch_extent + obs_cell
    blocks = obs_tile.shape[0]
    loc_matrix = jnp.sum(
        jnp.where(
            pattern[:, :, None] == jnp.arange(blocks, dtype=jnp.int32)[None, None, :],
            loc_weight[:, :, None],
            0.0,
        ),
        axis=1,
    )
    row_ids = jnp.arange(area_members, dtype=jnp.int32)
    tile_of_row = row_ids % tiles_dev
    earlier = row_ids[None, :] < row_ids[:, None]
    current = state
    mean_list = []
    for update_ordinal in range(CYCLES):
        moved = current.reshape(part_dev, strip_extent).astype(jnp.float32)
        for repeat in range(STEPS):
            padded = extended(moved, (("region", 1),), 1)
            moved = moved + smoothed_strip * (padded[:, :-2] - 2.0 * moved + padded[:, 2:])
        prior_ensemble = (
            moved
            + model_perturbation[update_ordinal].reshape(part_dev, strip_extent).astype(jnp.float32)
        ).astype(jnp.bfloat16)
        modelled_readings = prior_ensemble[:, measured_position].astype(jnp.float32)
        misses = obs_values[update_ordinal] - modelled_readings
        misfit = 0.5 * jnp.sum(obs_prec * misses * misses, axis=-1)
        loglik = jnp.dot(misfit, loc_matrix.T, precision=lax.Precision.HIGHEST)
        all_scores = lax.all_gather(loglik, "member", axis=0, tiled=True)
        lowest = jnp.min(all_scores, axis=0)
        totals = jnp.sum(jnp.exp(lowest - all_scores), axis=0)
        unscaled = jnp.exp(lowest - loglik)
        patch_member_slab = prior_ensemble.reshape(area_members, patch_extent)
        weighted = jnp.sum(
            unscaled[:, :, None]
            * patch_member_slab.reshape(part_dev, tiles_dev, patch_extent).astype(jnp.float32),
            axis=0,
        )
        portion = lax.psum_scatter(weighted, "member", scatter_dimension=1, tiled=True)
        mean_list.append(portion / totals[:, None])
        source = anc_member[update_ordinal, 0, :, :, 0].reshape(area_members)
        codes = anc_slot[update_ordinal, 0].reshape(area_members) * tiles_dev + tile_of_row
        ranks = jnp.sum((source[None, :] == source[:, None]) & earlier, axis=1)
        wanted = jnp.full((members, capacity), -1, jnp.int32).at[source, ranks].set(codes)
        fetched = patch_member_slab[
            jnp.maximum(
                lax.all_to_all(wanted, "member", split_axis=0, concat_axis=0, tiled=True), 0
            )
        ]
        arrived = lax.all_to_all(fetched, "member", split_axis=0, concat_axis=0, tiled=True)
        current = arrived[source, ranks].reshape(part_dev, tiles_dev, patch_extent)
    return (current, jnp.stack(mean_list))


def solution(mesh):
    in_specs = (
        P("member", "region", None),
        P("region", None),
        P(None, "member", "region", None),
        P(None, "region", None),
        P("region", None),
        P("region"),
        P("region", None),
        P("region", None),
        P("region", None),
        P(None, "region", "member", None, None),
        P(None, "region", "member", None),
    )
    out_specs = (P("member", "region", None), P(None, "region", "member"))
    return jax.shard_map(body, mesh=mesh, in_specs=in_specs, out_specs=out_specs, check_vma=False)
```

profile of v0, /device:TPU:0, one launch (start us, length us, event | category | flops | bytes accessed | tf_op | source)
XLA Modules:
  0.0 214.6 jit_solution(13415304741372341621)
XLA Ops:
  8.7 4.9 %collective-permute-start = (f32[2,1]{1,0:T(2,128)S(1)}, f32[2,1]{1,0:T(2,128)S(1)}, u32[]{:S(2)}, u32[]{:S(2)}) collective-permute-start(f32[2,1]{1,0:T(2,128)S(1)} %get-tuple-element.16), channel_id=1, source_target_pairs={{0,1},{1,2},{2,3},{4,5},{5,6},{6,7},{8,9},{9,10},{10,11},{12,13},{... | collective-permute-start | bytes 32 | tf_op jit(solution)/shard_map/ppermute | solution.py:17
  17.4 5.4 %scatter_fusion = s32[8,8]{1,0:T(8,128)} fusion(s32[8,8]{1,0:T(8,128)} %broadcast.129.clone.1, s32[32]{0:T(128)S(1)} %get-tuple-element.8, s32[32]{0:T(128)S(1)} %fusion.37), kind=kCustom, calls=%fused_computation.6 | custom fusion | bytes 640 | tf_op jit(solution)/shard_map/scatter | solution.py:85
  22.8 3.7 %all-to-all-start = ((s32[8,1,8]{2,1,0:T(1,128)}), s32[8,1,8]{2,1,0:T(1,128)S(1)}, u32[]{:S(2)}, u32[]{:S(2)}) async-start(s32[8,1,8]{2,1,0:T(1,128)} %bitcast.3), calls=%async_computation | async-start | bytes 8192 | tf_op jit(solution)/shard_map/all_to_all | solution.py:88
  32.0 5.4 %scatter_fusion.1 = s32[8,8]{1,0:T(8,128)} fusion(s32[8,8]{1,0:T(8,128)} %broadcast.129.clone, s32[32]{0:T(128)S(1)} %get-tuple-element.6, s32[32]{0:T(128)S(1)} %fusion.36), kind=kCustom, calls=%fused_computation.7 | custom fusion | bytes 640 | tf_op jit(solution)/shard_map/scatter | solution.py:85
  38.6 4.5 %collective-permute-start.2 = (f32[2,1]{1,0:T(2,128)S(1)}, f32[2,1]{1,0:T(2,128)S(1)}, u32[]{:S(2)}, u32[]{:S(2)}) collective-permute-start(f32[2,1]{1,0:T(2,128)S(1)} %get-tuple-element.14), channel_id=1, source_target_pairs={{0,1},{1,2},{2,3},{4,5},{5,6},{6,7},{8,9},{9,10},{10,11},{12,13},{... | collective-permute-start | bytes 32 | tf_op jit(solution)/shard_map/ppermute | solution.py:17
  44.5 4.2 %all-to-all-start.2 = ((s32[8,1,8]{2,1,0:T(1,128)}), s32[8,1,8]{2,1,0:T(1,128)S(1)}, u32[]{:S(2)}, u32[]{:S(2)}) async-start(s32[8,1,8]{2,1,0:T(1,128)} %bitcast.9), calls=%async_computation.2 | async-start | bytes 8192 | tf_op jit(solution)/shard_map/all_to_all | solution.py:88
  50.1 3.2 %all-to-all-done.2 = s32[8,1,8]{2,1,0:T(1,128)S(1)} async-done(((s32[8,1,8]{2,1,0:T(1,128)}), s32[8,1,8]{2,1,0:T(1,128)S(1)}, u32[]{:S(2)}, u32[]{:S(2)}) %all-to-all-start.2) | async-done | bytes 288 | tf_op jit(solution)/shard_map/all_to_all | solution.py:88
  53.4 1.7 gather_fusion
  55.0 3.5 %all-to-all-start.1 = ((bf16[8,8,4096]{2,1,0:T(8,128)(2,1)}), bf16[8,8,4096]{2,1,0:T(8,128)(2,1)S(1)}, u32[]{:S(2)}, u32[]{:S(2)}) async-start(bf16[8,8,4096]{2,1,0:T(8,128)(2,1)} %bitcast.4), calls=%async_computation.1 | async-start | bytes 1048576 | tf_op jit(solution)/shard_map/all_to_all | solution.py:91
  59.0 10.7 %copy.139 = bf16[2,65536]{0,1:T(8,128)(2,1)} copy(bf16[2,65536]{1,0:T(2,128)(2,1)S(1)} %fusion.18) | data formatting | bytes 524288 | tf_op jit(solution)/shard_map/convert_element_type | solution.py:65
  69.6 9.0 %gather_fusion.4 = bf16[512,2]{1,0:T(8,128)(2,1)S(1)} fusion(bf16[2,65536]{0,1:T(8,128)(2,1)} %copy.139, s32[1024]{0:T(1024)S(1)} %pad_clamp_fusion), kind=kCustom, calls=%fused_computation.4 | custom fusion | bytes 6144 | tf_op jit(solution)/shard_map/gather | solution.py:66
  80.7 4.5 %collective-permute-start.4 = (f32[2,1]{1,0:T(2,128)S(1)}, f32[2,1]{1,0:T(2,128)S(1)}, u32[]{:S(2)}, u32[]{:S(2)}) collective-permute-start(f32[2,1]{1,0:T(2,128)S(1)} %get-tuple-element.12), channel_id=1, source_target_pairs={{0,1},{1,2},{2,3},{4,5},{5,6},{6,7},{8,9},{9,10},{10,11},{12,13},{... | collective-permute-start | bytes 32 | tf_op jit(solution)/shard_map/ppermute | solution.py:17
  86.7 4.0 %collective-permute-done.5 = f32[2,1]{1,0:T(2,128)S(1)} collective-permute-done((f32[2,1]{1,0:T(2,128)S(1)}, f32[2,1]{1,0:T(2,128)S(1)}, u32[]{:S(2)}, u32[]{:S(2)}) %collective-permute-start.5) | collective-permute-done | bytes 40 | tf_op jit(solution)/shard_map/ppermute | solution.py:18
  91.9 3.5 %collective-permute-start.6 = (f32[2,1]{1,0:T(2,128)S(1)}, f32[2,1]{1,0:T(2,128)S(1)}, u32[]{:S(2)}, u32[]{:S(2)}) collective-permute-start(f32[2,1]{1,0:T(2,128)S(1)} %get-tuple-element.10), channel_id=1, source_target_pairs={{0,1},{1,2},{2,3},{4,5},{5,6},{6,7},{8,9},{9,10},{10,11},{12,13},{... | collective-permute-start | bytes 32 | tf_op jit(solution)/shard_map/ppermute | solution.py:17
  96.7 4.2 %collective-permute-done.7 = f32[2,1]{1,0:T(2,128)S(1)} collective-permute-done((f32[2,1]{1,0:T(2,128)S(1)}, f32[2,1]{1,0:T(2,128)S(1)}, u32[]{:S(2)}, u32[]{:S(2)}) %collective-permute-start.7) | collective-permute-done | bytes 40 | tf_op jit(solution)/shard_map/ppermute | solution.py:18
  102.1 10.7 %copy.141 = bf16[2,65536]{0,1:T(8,128)(2,1)} copy(bf16[2,65536]{1,0:T(2,128)(2,1)S(1)} %fusion.19) | data formatting | bytes 524288 | tf_op jit(solution)/shard_map/convert_element_type | solution.py:65
  112.7 9.0 %gather_fusion.5 = bf16[512,2]{1,0:T(8,128)(2,1)S(1)} fusion(bf16[2,65536]{0,1:T(8,128)(2,1)} %copy.141, s32[1024]{0:T(1024)S(1)} %pad_clamp_fusion), kind=kCustom, calls=%fused_computation.5 | custom fusion | bytes 6144 | tf_op jit(solution)/shard_map/gather | solution.py:66
  122.2 9.3 %all-gather = f32[8,2,16]{2,1,0:T(2,128)S(1)} all-gather(f32[1,2,16]{2,1,0:T(2,128)S(1)} %bitcast.95), channel_id=1, replica_groups=mesh['member'=8,'region'=4] {'member'}, dimensions={0}, use_global_device_ids=true | all-gather | bytes 1152 | tf_op jit(solution)/shard_map/all_gather | solution.py:70
  133.9 8.9 %all-gather.1 = f32[8,2,16]{2,1,0:T(2,128)S(1)} all-gather(f32[1,2,16]{2,1,0:T(2,128)S(1)} %bitcast.94), channel_id=1, replica_groups=mesh['member'=8,'region'=4] {'member'}, dimensions={0}, use_global_device_ids=true | all-gather | bytes 1152 | tf_op jit(solution)/shard_map/all_gather | solution.py:70
  145.2 1.7 gather_fusion.2
  146.9 3.5 %all-to-all-start.3 = ((bf16[8,8,4096]{2,1,0:T(8,128)(2,1)}), bf16[8,8,4096]{2,1,0:T(8,128)(2,1)S(1)}, u32[]{:S(2)}, u32[]{:S(2)}) async-start(bf16[8,8,4096]{2,1,0:T(8,128)(2,1)} %bitcast.10), calls=%async_computation.3 | async-start | bytes 1048576 | tf_op jit(solution)/shard_map/all_to_all | solution.py:91
  150.4 16.3 %reduce-scatter.3.cloned.1.call-done = f32[16,512]{1,0:T(8,128)} async-done(((f32[16,4096]{1,0:T(8,128)}), f32[16,512]{1,0:T(8,128)}) %reduce-scatter.3.cloned.1.call-update) | async-done | bytes 32784 | tf_op jit(solution)/shard_map/reduce_scatter | solution.py:80
  167.5 36.7 %reduce-scatter.5.cloned.1.call-done = f32[16,512]{1,0:T(8,128)} async-done(((f32[16,4096]{1,0:T(8,128)}), f32[16,512]{1,0:T(8,128)}) %reduce-scatter.5.cloned.1.call-update) | async-done | bytes 32784 | tf_op jit(solution)/shard_map/reduce_scatter | solution.py:80
  205.7 2.1 gather_fusion.3
  (94 shorter events, 29.9 us)
Async XLA Ops:
  7.2 51.4 %copy-start = (f32[2,32,16]{1,2,0:T(8,128)S(1)}, f32[2,32,16]{1,2,0:T(8,128)}, u32[]{:S(2)}) copy-start(f32[2,32,16]{1,2,0:T(8,128)} %param.14) | copy-start | bytes 12292
  7.2 51.6 %copy-start.1 = (f32[32,16]{0,1:T(8,128)S(1)}, f32[32,16]{0,1:T(8,128)}, u32[]{:S(2)}) copy-start(f32[32,16]{0,1:T(8,128)} %param.15) | copy-start | bytes 6148
  7.2 51.7 %copy-start.3 = (s32[16,6]{0,1:T(8,128)S(1)}, s32[16,6]{0,1:T(8,128)}, u32[]{:S(2)}) copy-start(s32[16,6]{0,1:T(8,128)} %param.18) | copy-start | bytes 1156
  7.2 51.7 %copy-start.2 = (f32[16,6]{0,1:T(8,128)S(1)}, f32[16,6]{0,1:T(8,128)}, u32[]{:S(2)}) copy-start(f32[16,6]{0,1:T(8,128)} %param.19) | copy-start | bytes 1156
  8.7 28.7 %collective-permute-start = (f32[2,1]{1,0:T(2,128)S(1)}, f32[2,1]{1,0:T(2,128)S(1)}, u32[]{:S(2)}, u32[]{:S(2)}) collective-permute-start(f32[2,1]{1,0:T(2,128)S(1)} %get-tuple-element.16), channel_id=1, source_target_pairs={{0,1},{1,2},{2,3},{4,5},{5,6},{6,7},{8,9},{9,10},{10,11},{12,13},{... | collective-permute-start | bytes 32 | tf_op jit(solution)/shard_map/ppermute | solution.py:17
  13.6 23.8 %collective-permute-start.1 = (f32[2,1]{1,0:T(2,128)S(1)}, f32[2,1]{1,0:T(2,128)S(1)}, u32[]{:S(2)}, u32[]{:S(2)}) collective-permute-start(f32[2,1]{1,0:T(2,128)S(1)} %get-tuple-element.17), channel_id=1, source_target_pairs={{1,0},{2,1},{3,2},{5,4},{6,5},{7,6},{9,8},{10,9},{11,10},{13,12},{... | collective-permute-start | bytes 32 | tf_op jit(solution)/shard_map/ppermute | solution.py:18
  22.8 21.7 %all-to-all-start = ((s32[8,1,8]{2,1,0:T(1,128)}), s32[8,1,8]{2,1,0:T(1,128)S(1)}, u32[]{:S(2)}, u32[]{:S(2)}) async-start(s32[8,1,8]{2,1,0:T(1,128)} %bitcast.3), calls=%async_computation | async-start | bytes 8192 | tf_op jit(solution)/shard_map/all_to_all | solution.py:88
  38.6 10.1 %collective-permute-start.2 = (f32[2,1]{1,0:T(2,128)S(1)}, f32[2,1]{1,0:T(2,128)S(1)}, u32[]{:S(2)}, u32[]{:S(2)}) collective-permute-start(f32[2,1]{1,0:T(2,128)S(1)} %get-tuple-element.14), channel_id=1, source_target_pairs={{0,1},{1,2},{2,3},{4,5},{5,6},{6,7},{8,9},{9,10},{10,11},{12,13},{... | collective-permute-start | bytes 32 | tf_op jit(solution)/shard_map/ppermute | solution.py:17
  43.2 5.5 %collective-permute-start.3 = (f32[2,1]{1,0:T(2,128)S(1)}, f32[2,1]{1,0:T(2,128)S(1)}, u32[]{:S(2)}, u32[]{:S(2)}) collective-permute-start(f32[2,1]{1,0:T(2,128)S(1)} %get-tuple-element.15), channel_id=1, source_target_pairs={{1,0},{2,1},{3,2},{5,4},{6,5},{7,6},{9,8},{10,9},{11,10},{13,12},{... | collective-permute-start | bytes 32 | tf_op jit(solution)/shard_map/ppermute | solution.py:18
  44.5 8.8 %all-to-all-start.2 = ((s32[8,1,8]{2,1,0:T(1,128)}), s32[8,1,8]{2,1,0:T(1,128)S(1)}, u32[]{:S(2)}, u32[]{:S(2)}) async-start(s32[8,1,8]{2,1,0:T(1,128)} %bitcast.9), calls=%async_computation.2 | async-start | bytes 8192 | tf_op jit(solution)/shard_map/all_to_all | solution.py:88
  55.0 23.7 %all-to-all-start.1 = ((bf16[8,8,4096]{2,1,0:T(8,128)(2,1)}), bf16[8,8,4096]{2,1,0:T(8,128)(2,1)S(1)}, u32[]{:S(2)}, u32[]{:S(2)}) async-start(bf16[8,8,4096]{2,1,0:T(8,128)(2,1)} %bitcast.4), calls=%async_computation.1 | async-start | bytes 1048576 | tf_op jit(solution)/shard_map/all_to_all | solution.py:91
  58.5 108.1 %reduce-scatter.3.cloned.1.call-start = ((), (), s32[]{:S(2)}) async-start(), calls=%async_computation.6 | async-start | bytes 294912 | tf_op jit(solution)/shard_map/reduce_scatter | solution.py:80
  80.7 6.0 %collective-permute-start.4 = (f32[2,1]{1,0:T(2,128)S(1)}, f32[2,1]{1,0:T(2,128)S(1)}, u32[]{:S(2)}, u32[]{:S(2)}) collective-permute-start(f32[2,1]{1,0:T(2,128)S(1)} %get-tuple-element.12), channel_id=1, source_target_pairs={{0,1},{1,2},{2,3},{4,5},{5,6},{6,7},{8,9},{9,10},{10,11},{12,13},{... | collective-permute-start | bytes 32 | tf_op jit(solution)/shard_map/ppermute | solution.py:17
  85.2 5.5 %collective-permute-start.5 = (f32[2,1]{1,0:T(2,128)S(1)}, f32[2,1]{1,0:T(2,128)S(1)}, u32[]{:S(2)}, u32[]{:S(2)}) collective-permute-start(f32[2,1]{1,0:T(2,128)S(1)} %get-tuple-element.13), channel_id=1, source_target_pairs={{1,0},{2,1},{3,2},{5,4},{6,5},{7,6},{9,8},{10,9},{11,10},{13,12},{... | collective-permute-start | bytes 32 | tf_op jit(solution)/shard_map/ppermute | solution.py:18
  91.9 4.8 %collective-permute-start.6 = (f32[2,1]{1,0:T(2,128)S(1)}, f32[2,1]{1,0:T(2,128)S(1)}, u32[]{:S(2)}, u32[]{:S(2)}) collective-permute-start(f32[2,1]{1,0:T(2,128)S(1)} %get-tuple-element.10), channel_id=1, source_target_pairs={{0,1},{1,2},{2,3},{4,5},{5,6},{6,7},{8,9},{9,10},{10,11},{12,13},{... | collective-permute-start | bytes 32 | tf_op jit(solution)/shard_map/ppermute | solution.py:17
  95.4 5.5 %collective-permute-start.7 = (f32[2,1]{1,0:T(2,128)S(1)}, f32[2,1]{1,0:T(2,128)S(1)}, u32[]{:S(2)}, u32[]{:S(2)}) collective-permute-start(f32[2,1]{1,0:T(2,128)S(1)} %get-tuple-element.11), channel_id=1, source_target_pairs={{1,0},{2,1},{3,2},{5,4},{6,5},{7,6},{9,8},{10,9},{11,10},{13,12},{... | collective-permute-start | bytes 32 | tf_op jit(solution)/shard_map/ppermute | solution.py:18
  133.7 70.5 %reduce-scatter.5.cloned.1.call-start = ((), (), s32[]{:S(2)}) async-start(), calls=%async_computation.7 | async-start | bytes 294912 | tf_op jit(solution)/shard_map/reduce_scatter | solution.py:80
  146.9 58.8 %all-to-all-start.3 = ((bf16[8,8,4096]{2,1,0:T(8,128)(2,1)}), bf16[8,8,4096]{2,1,0:T(8,128)(2,1)S(1)}, u32[]{:S(2)}, u32[]{:S(2)}) async-start(bf16[8,8,4096]{2,1,0:T(8,128)(2,1)} %bitcast.10), calls=%async_computation.3 | async-start | bytes 1048576 | tf_op jit(solution)/shard_map/all_to_all | solution.py:91
Sparse Core Ops, SparseCore 0:
  133.8 32.8 reduce-scatter.2
  170.6 33.5 reduce-scatter.4
where the time goes:
time: 216 us; the launch traced here: 215 us
  local copies, waits for them, and re-layouts  65.8 us (30%)
  waiting for transfers between devices  64.3 us (30%)
  starting transfers between devices  37.8 us (17%)
  blocking collectives  18.1 us (8%)
  between operations  14.4 us (7%)
  other arithmetic  13.8 us (6%)
    reduce_scatter x2, waiting for transfers between devices, body(): lax.psum_scatter(weighted, 'member', scatter_dimension=1, tiled=True)  52.9 us
    convert_element_type x2, local copies, waits for them, and re-layouts, body(): prior_ensemble = (moved + model_perturbation[update_ordinal].reshape(part...  21.3 us
    all_gather x2, blocking collectives, body(): all_scores = lax.all_gather(loglik, 'member', axis=0, tiled=True)  18.1 us
    gather x2, local copies, waits for them, and re-layouts, body(): modelled_readings = prior_ensemble[:, measured_position].astype(jnp.float32)  18 us
    ppermute x4, starting transfers between devices, extended(): before = lax.ppermute(last, axis, up)  17.5 us
    scatter x2, local copies, waits for them, and re-layouts, body(): jnp.full((members, capacity), -1, jnp.int32).at[source, ranks].set(codes)  10.8 us
    ppermute x4, waiting for transfers between devices, extended(): after = lax.ppermute(initial, axis, down)  8.13 us
    all_to_all x2, starting transfers between devices, body(): lax.all_to_all(wanted, 'member', split_axis=0, concat_axis=0, tiled=True)  7.93 us
  transfers between devices with their start and end apart: 14, of which 5 were waited for; matrix products, arithmetic and copies ran while one was open for 22% of the time, Pallas kernels for 0%

commit v1 on v0

--- a/solution.py
+++ b/solution.py
@@ -67,7 +67,16 @@
         misses = obs_values[update_ordinal] - modelled_readings
         misfit = 0.5 * jnp.sum(obs_prec * misses * misses, axis=-1)
         loglik = jnp.dot(misfit, loc_matrix.T, precision=lax.Precision.HIGHEST)
-        all_scores = lax.all_gather(loglik, "member", axis=0, tiled=True)
+        ring = [loglik]
+        for hop in range(7):
+            ring.append(
+                lax.ppermute(ring[-1], "member", [(dev, (dev + 1) % 8) for dev in range(8)])
+            )
+        all_scores = jnp.roll(
+            jnp.concatenate(ring[::-1], axis=0),
+            (lax.axis_index("member") + 1) * ring[0].shape[0],
+            axis=0,
+        )
         lowest = jnp.min(all_scores, axis=0)
         totals = jnp.sum(jnp.exp(lowest - all_scores), axis=0)
         unscaled = jnp.exp(lowest - loglik)

time: 216 us -> 241 us (1.12)
  waiting for transfers between devices: 64.3 us -> 103 us
  blocking collectives: 18.1 us -> 0 us
  starting transfers between devices: 37.8 us -> 41.9 us
    ppermute x0 -> x14, waiting for transfers between devices: none -> 26.6 us  [body(): lax.ppermute(ring[-1], 'member', [(dev, (dev + 1) % 8) for dev in range(8)])]
    all_gather x2 -> x0, blocking collectives: 18.1 us -> none  [body(): all_scores = lax.all_gather(loglik, 'member', axis=0, tiled=True)]
    reduce_scatter x2, waiting for transfers between devices: 52.9 us -> 65.4 us  [body(): lax.psum_scatter(weighted, 'member', scatter_dimension=1, tiled=True)]
    ppermute x0 -> x14, starting transfers between devices: none -> 4.09 us  [body(): lax.ppermute(ring[-1], 'member', [(dev, (dev + 1) % 8) for dev in range(8)])]
  transfers between devices with their start and end apart: 14 -> 28, of which waited for: 5 -> 15; matrix products, arithmetic and copies ran while one was open for 22% -> 21% of each run, Pallas kernels for 0% -> 0%
where the time goes in v1:
time: 241 us; the launch traced here: 240 us
  waiting for transfers between devices  103 us (43%)
  local copies, waits for them, and re-layouts  65.9 us (27%)
  starting transfers between devices  41.9 us (17%)
  between operations  14.4 us (6%)
  other arithmetic  13.8 us (6%)
    reduce_scatter x2, waiting for transfers between devices, body(): lax.psum_scatter(weighted, 'member', scatter_dimension=1, tiled=True)  65.4 us
    ppermute x14, waiting for transfers between devices, body(): lax.ppermute(ring[-1], 'member', [(dev, (dev + 1) % 8) for dev in range(8)])  26.6 us
    convert_element_type x2, local copies, waits for them, and re-layouts, body(): prior_ensemble = (moved + model_perturbation[update_ordinal].reshape(part...  21.3 us
    gather x2, local copies, waits for them, and re-layouts, body(): modelled_readings = prior_ensemble[:, measured_position].astype(jnp.float32)  18 us
    ppermute x4, starting transfers between devices, extended(): before = lax.ppermute(last, axis, up)  17.5 us
    scatter x2, local copies, waits for them, and re-layouts, body(): jnp.full((members, capacity), -1, jnp.int32).at[source, ranks].set(codes)  10.8 us
    ppermute x4, waiting for transfers between devices, extended(): after = lax.ppermute(initial, axis, down)  8.13 us
    all_to_all x2, starting transfers between devices, body(): lax.all_to_all(wanted, 'member', split_axis=0, concat_axis=0, tiled=True)  7.93 us
  transfers between devices with their start and end apart: 28, of which 15 were waited for; matrix products, arithmetic and copies ran while one was open for 21% of the time, Pallas kernels for 0%

profile of v1, /device:TPU:0, one launch (start us, length us, event | category | flops | bytes accessed | tf_op | source)
XLA Modules:
  0.0 239.8 jit_solution(5055049928774001116)
XLA Ops:
  8.7 4.9 %collective-permute-start = (f32[2,1]{1,0:T(2,128)S(1)}, f32[2,1]{1,0:T(2,128)S(1)}, u32[]{:S(2)}, u32[]{:S(2)}) collective-permute-start(f32[2,1]{1,0:T(2,128)S(1)} %get-tuple-element.17), channel_id=1, source_target_pairs={{0,1},{1,2},{2,3},{4,5},{5,6},{6,7},{8,9},{9,10},{10,11},{12,13},{... | collective-permute-start | bytes 32 | tf_op jit(solution)/shard_map/ppermute | solution.py:17
  17.4 5.4 %scatter_fusion = s32[8,8]{1,0:T(8,128)} fusion(s32[8,8]{1,0:T(8,128)} %broadcast.130.clone.1, s32[32]{0:T(128)S(1)} %get-tuple-element.9, s32[32]{0:T(128)S(1)} %fusion.41), kind=kCustom, calls=%fused_computation.6 | custom fusion | bytes 640 | tf_op jit(solution)/shard_map/scatter | solution.py:94
  22.8 3.7 %all-to-all-start = ((s32[8,1,8]{2,1,0:T(1,128)}), s32[8,1,8]{2,1,0:T(1,128)S(1)}, u32[]{:S(2)}, u32[]{:S(2)}) async-start(s32[8,1,8]{2,1,0:T(1,128)} %bitcast.3), calls=%async_computation | async-start | bytes 8192 | tf_op jit(solution)/shard_map/all_to_all | solution.py:97
  32.0 5.4 %scatter_fusion.1 = s32[8,8]{1,0:T(8,128)} fusion(s32[8,8]{1,0:T(8,128)} %broadcast.130.clone, s32[32]{0:T(128)S(1)} %get-tuple-element.7, s32[32]{0:T(128)S(1)} %fusion.40), kind=kCustom, calls=%fused_computation.7 | custom fusion | bytes 640 | tf_op jit(solution)/shard_map/scatter | solution.py:94
  38.6 4.5 %collective-permute-start.2 = (f32[2,1]{1,0:T(2,128)S(1)}, f32[2,1]{1,0:T(2,128)S(1)}, u32[]{:S(2)}, u32[]{:S(2)}) collective-permute-start(f32[2,1]{1,0:T(2,128)S(1)} %get-tuple-element.15), channel_id=1, source_target_pairs={{0,1},{1,2},{2,3},{4,5},{5,6},{6,7},{8,9},{9,10},{10,11},{12,13},{... | collective-permute-start | bytes 32 | tf_op jit(solution)/shard_map/ppermute | solution.py:17
  44.5 4.2 %all-to-all-start.2 = ((s32[8,1,8]{2,1,0:T(1,128)}), s32[8,1,8]{2,1,0:T(1,128)S(1)}, u32[]{:S(2)}, u32[]{:S(2)}) async-start(s32[8,1,8]{2,1,0:T(1,128)} %bitcast.9), calls=%async_computation.2 | async-start | bytes 8192 | tf_op jit(solution)/shard_map/all_to_all | solution.py:97
  55.0 3.5 %all-to-all-start.1 = ((bf16[8,8,4096]{2,1,0:T(8,128)(2,1)}), bf16[8,8,4096]{2,1,0:T(8,128)(2,1)S(1)}, u32[]{:S(2)}, u32[]{:S(2)}) async-start(bf16[8,8,4096]{2,1,0:T(8,128)(2,1)} %bitcast.4), calls=%async_computation.1 | async-start | bytes 1048576 | tf_op jit(solution)/shard_map/all_to_all | solution.py:100
  58.9 10.7 %copy.139 = bf16[2,65536]{0,1:T(8,128)(2,1)} copy(bf16[2,65536]{1,0:T(2,128)(2,1)S(1)} %fusion.18) | data formatting | bytes 524288 | tf_op jit(solution)/shard_map/convert_element_type | solution.py:65
  69.6 9.0 %gather_fusion.4 = bf16[512,2]{1,0:T(8,128)(2,1)S(1)} fusion(bf16[2,65536]{0,1:T(8,128)(2,1)} %copy.139, s32[1024]{0:T(1024)S(1)} %pad_clamp_fusion), kind=kCustom, calls=%fused_computation.4 | custom fusion | bytes 6144 | tf_op jit(solution)/shard_map/gather | solution.py:66
  80.7 4.6 %collective-permute-start.4 = (f32[2,1]{1,0:T(2,128)S(1)}, f32[2,1]{1,0:T(2,128)S(1)}, u32[]{:S(2)}, u32[]{:S(2)}) collective-permute-start(f32[2,1]{1,0:T(2,128)S(1)} %get-tuple-element.13), channel_id=1, source_target_pairs={{0,1},{1,2},{2,3},{4,5},{5,6},{6,7},{8,9},{9,10},{10,11},{12,13},{... | collective-permute-start | bytes 32 | tf_op jit(solution)/shard_map/ppermute | solution.py:17
  86.7 4.0 %collective-permute-done.5 = f32[2,1]{1,0:T(2,128)S(1)} collective-permute-done((f32[2,1]{1,0:T(2,128)S(1)}, f32[2,1]{1,0:T(2,128)S(1)}, u32[]{:S(2)}, u32[]{:S(2)}) %collective-permute-start.5) | collective-permute-done | bytes 40 | tf_op jit(solution)/shard_map/ppermute | solution.py:18
  91.9 3.5 %collective-permute-start.6 = (f32[2,1]{1,0:T(2,128)S(1)}, f32[2,1]{1,0:T(2,128)S(1)}, u32[]{:S(2)}, u32[]{:S(2)}) collective-permute-start(f32[2,1]{1,0:T(2,128)S(1)} %get-tuple-element.11), channel_id=1, source_target_pairs={{0,1},{1,2},{2,3},{4,5},{5,6},{6,7},{8,9},{9,10},{10,11},{12,13},{... | collective-permute-start | bytes 32 | tf_op jit(solution)/shard_map/ppermute | solution.py:17
  96.7 4.2 %collective-permute-done.7 = f32[2,1]{1,0:T(2,128)S(1)} collective-permute-done((f32[2,1]{1,0:T(2,128)S(1)}, f32[2,1]{1,0:T(2,128)S(1)}, u32[]{:S(2)}, u32[]{:S(2)}) %collective-permute-start.7) | collective-permute-done | bytes 40 | tf_op jit(solution)/shard_map/ppermute | solution.py:18
  102.0 10.7 %copy.141 = bf16[2,65536]{0,1:T(8,128)(2,1)} copy(bf16[2,65536]{1,0:T(2,128)(2,1)S(1)} %fusion.19) | data formatting | bytes 524288 | tf_op jit(solution)/shard_map/convert_element_type | solution.py:65
  112.9 9.0 %gather_fusion.5 = bf16[512,2]{1,0:T(8,128)(2,1)S(1)} fusion(bf16[2,65536]{0,1:T(8,128)(2,1)} %copy.141, s32[1024]{0:T(1024)S(1)} %pad_clamp_fusion), kind=kCustom, calls=%fused_computation.5 | custom fusion | bytes 6144 | tf_op jit(solution)/shard_map/gather | solution.py:66
  126.3 3.5 %all-to-all-start.3 = ((bf16[8,8,4096]{2,1,0:T(8,128)(2,1)}), bf16[8,8,4096]{2,1,0:T(8,128)(2,1)S(1)}, u32[]{:S(2)}, u32[]{:S(2)}) async-start(bf16[8,8,4096]{2,1,0:T(8,128)(2,1)} %bitcast.10), calls=%async_computation.3 | async-start | bytes 1048576 | tf_op jit(solution)/shard_map/all_to_all | solution.py:100
  131.9 7.2 %collective-permute-done.9 = f32[2,16]{1,0:T(2,128)S(1)} collective-permute-done((f32[2,16]{1,0:T(2,128)S(1)}, f32[2,16]{1,0:T(2,128)S(1)}, u32[]{:S(2)}, u32[]{:S(2)}) %collective-permute-start.9) | collective-permute-done | bytes 160 | tf_op jit(solution)/shard_map/ppermute | solution.py:73
  139.1 3.9 %collective-permute-done.10 = f32[2,16]{1,0:T(2,128)S(1)} collective-permute-done((f32[2,16]{1,0:T(2,128)S(1)}, f32[2,16]{1,0:T(2,128)S(1)}, u32[]{:S(2)}, u32[]{:S(2)}) %collective-permute-start.10) | collective-permute-done | bytes 160 | tf_op jit(solution)/shard_map/ppermute | solution.py:73
  143.0 3.8 %collective-permute-done.11 = f32[2,16]{1,0:T(2,128)S(1)} collective-permute-done((f32[2,16]{1,0:T(2,128)S(1)}, f32[2,16]{1,0:T(2,128)S(1)}, u32[]{:S(2)}, u32[]{:S(2)}) %collective-permute-start.11) | collective-permute-done | bytes 160 | tf_op jit(solution)/shard_map/ppermute | solution.py:73
  146.9 3.8 %collective-permute-done.12 = f32[2,16]{1,0:T(2,128)S(1)} collective-permute-done((f32[2,16]{1,0:T(2,128)S(1)}, f32[2,16]{1,0:T(2,128)S(1)}, u32[]{:S(2)}, u32[]{:S(2)}) %collective-permute-start.12) | collective-permute-done | bytes 160 | tf_op jit(solution)/shard_map/ppermute | solution.py:73
  150.8 3.8 %collective-permute-done.13 = f32[2,16]{1,0:T(2,128)S(1)} collective-permute-done((f32[2,16]{1,0:T(2,128)S(1)}, f32[2,16]{1,0:T(2,128)S(1)}, u32[]{:S(2)}, u32[]{:S(2)}) %collective-permute-start.13) | collective-permute-done | bytes 160 | tf_op jit(solution)/shard_map/ppermute | solution.py:73
  154.7 3.8 %collective-permute-done.14 = f32[2,16]{1,0:T(2,128)S(1)} collective-permute-done((f32[2,16]{1,0:T(2,128)S(1)}, f32[2,16]{1,0:T(2,128)S(1)}, u32[]{:S(2)}, u32[]{:S(2)}) %collective-permute-start.14) | collective-permute-done | bytes 160 | tf_op jit(solution)/shard_map/ppermute | solution.py:73
  163.2 28.7 %reduce-scatter.3.cloned.1.call-done = f32[16,512]{1,0:T(8,128)} async-done(((f32[16,4096]{1,0:T(8,128)}), f32[16,512]{1,0:T(8,128)}) %reduce-scatter.3.cloned.1.call-update) | async-done | bytes 32784 | tf_op jit(solution)/shard_map/reduce_scatter | solution.py:89
  192.7 36.7 %reduce-scatter.5.cloned.1.call-done = f32[16,512]{1,0:T(8,128)} async-done(((f32[16,4096]{1,0:T(8,128)}), f32[16,512]{1,0:T(8,128)}) %reduce-scatter.5.cloned.1.call-update) | async-done | bytes 32784 | tf_op jit(solution)/shard_map/reduce_scatter | solution.py:89
  (122 shorter events, 43.1 us)
Async XLA Ops:
  8.7 28.7 %collective-permute-start = (f32[2,1]{1,0:T(2,128)S(1)}, f32[2,1]{1,0:T(2,128)S(1)}, u32[]{:S(2)}, u32[]{:S(2)}) collective-permute-start(f32[2,1]{1,0:T(2,128)S(1)} %get-tuple-element.17), channel_id=1, source_target_pairs={{0,1},{1,2},{2,3},{4,5},{5,6},{6,7},{8,9},{9,10},{10,11},{12,13},{... | collective-permute-start | bytes 32 | tf_op jit(solution)/shard_map/ppermute | solution.py:17
  13.6 23.8 %collective-permute-start.1 = (f32[2,1]{1,0:T(2,128)S(1)}, f32[2,1]{1,0:T(2,128)S(1)}, u32[]{:S(2)}, u32[]{:S(2)}) collective-permute-start(f32[2,1]{1,0:T(2,128)S(1)} %get-tuple-element.18), channel_id=1, source_target_pairs={{1,0},{2,1},{3,2},{5,4},{6,5},{7,6},{9,8},{10,9},{11,10},{13,12},{... | collective-permute-start | bytes 32 | tf_op jit(solution)/shard_map/ppermute | solution.py:18
  22.8 21.7 %all-to-all-start = ((s32[8,1,8]{2,1,0:T(1,128)}), s32[8,1,8]{2,1,0:T(1,128)S(1)}, u32[]{:S(2)}, u32[]{:S(2)}) async-start(s32[8,1,8]{2,1,0:T(1,128)} %bitcast.3), calls=%async_computation | async-start | bytes 8192 | tf_op jit(solution)/shard_map/all_to_all | solution.py:97
  38.6 10.1 %collective-permute-start.2 = (f32[2,1]{1,0:T(2,128)S(1)}, f32[2,1]{1,0:T(2,128)S(1)}, u32[]{:S(2)}, u32[]{:S(2)}) collective-permute-start(f32[2,1]{1,0:T(2,128)S(1)} %get-tuple-element.15), channel_id=1, source_target_pairs={{0,1},{1,2},{2,3},{4,5},{5,6},{6,7},{8,9},{9,10},{10,11},{12,13},{... | collective-permute-start | bytes 32 | tf_op jit(solution)/shard_map/ppermute | solution.py:17
  43.2 5.5 %collective-permute-start.3 = (f32[2,1]{1,0:T(2,128)S(1)}, f32[2,1]{1,0:T(2,128)S(1)}, u32[]{:S(2)}, u32[]{:S(2)}) collective-permute-start(f32[2,1]{1,0:T(2,128)S(1)} %get-tuple-element.16), channel_id=1, source_target_pairs={{1,0},{2,1},{3,2},{5,4},{6,5},{7,6},{9,8},{10,9},{11,10},{13,12},{... | collective-permute-start | bytes 32 | tf_op jit(solution)/shard_map/ppermute | solution.py:18
  44.5 8.8 %all-to-all-start.2 = ((s32[8,1,8]{2,1,0:T(1,128)}), s32[8,1,8]{2,1,0:T(1,128)S(1)}, u32[]{:S(2)}, u32[]{:S(2)}) async-start(s32[8,1,8]{2,1,0:T(1,128)} %bitcast.9), calls=%async_computation.2 | async-start | bytes 8192 | tf_op jit(solution)/shard_map/all_to_all | solution.py:97
  55.0 23.6 %all-to-all-start.1 = ((bf16[8,8,4096]{2,1,0:T(8,128)(2,1)}), bf16[8,8,4096]{2,1,0:T(8,128)(2,1)S(1)}, u32[]{:S(2)}, u32[]{:S(2)}) async-start(bf16[8,8,4096]{2,1,0:T(8,128)(2,1)} %bitcast.4), calls=%async_computation.1 | async-start | bytes 1048576 | tf_op jit(solution)/shard_map/all_to_all | solution.py:100
  80.7 6.1 %collective-permute-start.4 = (f32[2,1]{1,0:T(2,128)S(1)}, f32[2,1]{1,0:T(2,128)S(1)}, u32[]{:S(2)}, u32[]{:S(2)}) collective-permute-start(f32[2,1]{1,0:T(2,128)S(1)} %get-tuple-element.13), channel_id=1, source_target_pairs={{0,1},{1,2},{2,3},{4,5},{5,6},{6,7},{8,9},{9,10},{10,11},{12,13},{... | collective-permute-start | bytes 32 | tf_op jit(solution)/shard_map/ppermute | solution.py:17
  85.2 5.5 %collective-permute-start.5 = (f32[2,1]{1,0:T(2,128)S(1)}, f32[2,1]{1,0:T(2,128)S(1)}, u32[]{:S(2)}, u32[]{:S(2)}) collective-permute-start(f32[2,1]{1,0:T(2,128)S(1)} %get-tuple-element.14), channel_id=1, source_target_pairs={{1,0},{2,1},{3,2},{5,4},{6,5},{7,6},{9,8},{10,9},{11,10},{13,12},{... | collective-permute-start | bytes 32 | tf_op jit(solution)/shard_map/ppermute | solution.py:18
  91.9 4.8 %collective-permute-start.6 = (f32[2,1]{1,0:T(2,128)S(1)}, f32[2,1]{1,0:T(2,128)S(1)}, u32[]{:S(2)}, u32[]{:S(2)}) collective-permute-start(f32[2,1]{1,0:T(2,128)S(1)} %get-tuple-element.11), channel_id=1, source_target_pairs={{0,1},{1,2},{2,3},{4,5},{5,6},{6,7},{8,9},{9,10},{10,11},{12,13},{... | collective-permute-start | bytes 32 | tf_op jit(solution)/shard_map/ppermute | solution.py:17
  95.4 5.5 %collective-permute-start.7 = (f32[2,1]{1,0:T(2,128)S(1)}, f32[2,1]{1,0:T(2,128)S(1)}, u32[]{:S(2)}, u32[]{:S(2)}) collective-permute-start(f32[2,1]{1,0:T(2,128)S(1)} %get-tuple-element.12), channel_id=1, source_target_pairs={{1,0},{2,1},{3,2},{5,4},{6,5},{7,6},{9,8},{10,9},{11,10},{13,12},{... | collective-permute-start | bytes 32 | tf_op jit(solution)/shard_map/ppermute | solution.py:18
  122.4 7.4 %collective-permute-start.8 = (f32[2,16]{1,0:T(2,128)S(1)}, f32[2,16]{1,0:T(2,128)S(1)}, u32[]{:S(2)}, u32[]{:S(2)}) collective-permute-start(f32[2,16]{1,0:T(2,128)S(1)} %fusion.26), channel_id=1, source_target_pairs={{0,4},{4,8},{8,12},{12,16},{16,20},{20,24},{24,28},{28,0},{1,5},{5... | collective-permute-start | bytes 392 | tf_op jit(solution)/shard_map/ppermute | solution.py:73
  122.6 7.6 %collective-permute-start.15 = (f32[2,16]{1,0:T(2,128)S(1)}, f32[2,16]{1,0:T(2,128)S(1)}, u32[]{:S(2)}, u32[]{:S(2)}) collective-permute-start(f32[2,16]{1,0:T(2,128)S(1)} %fusion.24), channel_id=1, source_target_pairs={{0,4},{4,8},{8,12},{12,16},{16,20},{20,24},{24,28},{28,0},{1,5},{5... | collective-permute-start | bytes 392 | tf_op jit(solution)/shard_map/ppermute | solution.py:73
  126.3 104.6 %all-to-all-start.3 = ((bf16[8,8,4096]{2,1,0:T(8,128)(2,1)}), bf16[8,8,4096]{2,1,0:T(8,128)(2,1)S(1)}, u32[]{:S(2)}, u32[]{:S(2)}) async-start(bf16[8,8,4096]{2,1,0:T(8,128)(2,1)} %bitcast.10), calls=%async_computation.3 | async-start | bytes 1048576 | tf_op jit(solution)/shard_map/all_to_all | solution.py:100
  129.8 62.1 %reduce-scatter.3.cloned.1.call-start = ((), (), s32[]{:S(2)}) async-start(), calls=%async_computation.6 | async-start | bytes 294912 | tf_op jit(solution)/shard_map/reduce_scatter | solution.py:89
  129.9 9.2 %collective-permute-start.9 = (f32[2,16]{1,0:T(2,128)S(1)}, f32[2,16]{1,0:T(2,128)S(1)}, u32[]{:S(2)}, u32[]{:S(2)}) collective-permute-start(f32[2,16]{1,0:T(2,128)S(1)} %collective-permute-done.8), channel_id=1, source_target_pairs={{0,4},{4,8},{8,12},{12,16},{16,20},{20,24},{24,28},{28,0},{1,5},{5... | collective-permute-start | bytes 392 | tf_op jit(solution)/shard_map/ppermute | solution.py:73
  130.3 8.8 %collective-permute-start.16 = (f32[2,16]{1,0:T(2,128)S(1)}, f32[2,16]{1,0:T(2,128)S(1)}, u32[]{:S(2)}, u32[]{:S(2)}) collective-permute-start(f32[2,16]{1,0:T(2,128)S(1)} %collective-permute-done.15), channel_id=1, source_target_pairs={{0,4},{4,8},{8,12},{12,16},{16,20},{20,24},{24,28},{28,0},{1,5},{5... | collective-permute-start | bytes 392 | tf_op jit(solution)/shard_map/ppermute | solution.py:73
  139.1 3.9 %collective-permute-start.10 = (f32[2,16]{1,0:T(2,128)S(1)}, f32[2,16]{1,0:T(2,128)S(1)}, u32[]{:S(2)}, u32[]{:S(2)}) collective-permute-start(f32[2,16]{1,0:T(2,128)S(1)} %collective-permute-done.9), channel_id=1, source_target_pairs={{0,4},{4,8},{8,12},{12,16},{16,20},{20,24},{24,28},{28,0},{1,5},{5... | collective-permute-start | bytes 392 | tf_op jit(solution)/shard_map/ppermute | solution.py:73
  139.1 3.9 %collective-permute-start.17 = (f32[2,16]{1,0:T(2,128)S(1)}, f32[2,16]{1,0:T(2,128)S(1)}, u32[]{:S(2)}, u32[]{:S(2)}) collective-permute-start(f32[2,16]{1,0:T(2,128)S(1)} %collective-permute-done.16), channel_id=1, source_target_pairs={{0,4},{4,8},{8,12},{12,16},{16,20},{20,24},{24,28},{28,0},{1,5},{5... | collective-permute-start | bytes 392 | tf_op jit(solution)/shard_map/ppermute | solution.py:73
  146.8 3.9 %collective-permute-start.12 = (f32[2,16]{1,0:T(2,128)S(1)}, f32[2,16]{1,0:T(2,128)S(1)}, u32[]{:S(2)}, u32[]{:S(2)}) collective-permute-start(f32[2,16]{1,0:T(2,128)S(1)} %collective-permute-done.11), channel_id=1, source_target_pairs={{0,4},{4,8},{8,12},{12,16},{16,20},{20,24},{24,28},{28,0},{1,5},{5... | collective-permute-start | bytes 392 | tf_op jit(solution)/shard_map/ppermute | solution.py:73
  146.9 3.9 %collective-permute-start.19 = (f32[2,16]{1,0:T(2,128)S(1)}, f32[2,16]{1,0:T(2,128)S(1)}, u32[]{:S(2)}, u32[]{:S(2)}) collective-permute-start(f32[2,16]{1,0:T(2,128)S(1)} %collective-permute-done.18), channel_id=1, source_target_pairs={{0,4},{4,8},{8,12},{12,16},{16,20},{20,24},{24,28},{28,0},{1,5},{5... | collective-permute-start | bytes 392 | tf_op jit(solution)/shard_map/ppermute | solution.py:73
  150.7 3.9 %collective-permute-start.13 = (f32[2,16]{1,0:T(2,128)S(1)}, f32[2,16]{1,0:T(2,128)S(1)}, u32[]{:S(2)}, u32[]{:S(2)}) collective-permute-start(f32[2,16]{1,0:T(2,128)S(1)} %collective-permute-done.12), channel_id=1, source_target_pairs={{0,4},{4,8},{8,12},{12,16},{16,20},{20,24},{24,28},{28,0},{1,5},{5... | collective-permute-start | bytes 392 | tf_op jit(solution)/shard_map/ppermute | solution.py:73
  154.7 6.1 %collective-permute-start.21 = (f32[2,16]{1,0:T(2,128)S(1)}, f32[2,16]{1,0:T(2,128)S(1)}, u32[]{:S(2)}, u32[]{:S(2)}) collective-permute-start(f32[2,16]{1,0:T(2,128)S(1)} %collective-permute-done.20), channel_id=1, source_target_pairs={{0,4},{4,8},{8,12},{12,16},{16,20},{20,24},{24,28},{28,0},{1,5},{5... | collective-permute-start | bytes 392 | tf_op jit(solution)/shard_map/ppermute | solution.py:73
  160.8 68.6 %reduce-scatter.5.cloned.1.call-start = ((), (), s32[]{:S(2)}) async-start(), calls=%async_computation.7 | async-start | bytes 294912 | tf_op jit(solution)/shard_map/reduce_scatter | solution.py:89
  (8 other events, 221.7 us)
Sparse Core Ops, SparseCore 0:
  160.9 30.9 reduce-scatter.2
  195.8 33.5 reduce-scatter.4
